TPU v7x, 256 devices: a whole 4x4x8 slice. The times are simulated.
256 devices in a mesh: wide: 64 (over y, z, core), narrow: 4 (over x).
Axes of the slice: x: 4, y: 4, z: 8, core: 2. Of those that a mesh axis runs over, the one named last changes fastest.
Arguments:
- embedding: float32 [131072, 128], P(('wide', 'narrow'))
- tile_blocks: bfloat16 [64, 4, 22, 512, 512], P('wide', 'narrow'), may hold values from -0.125 to 0.125
- tile_row: int32 [64, 4, 22], P('wide', 'narrow'), may hold values from 0 to 3
- tile_col: int32 [64, 4, 22], P('wide', 'narrow'), may hold values from 0 to 63
- counts: int32 [64, 4], P('wide', 'narrow'), may hold values from 1 to 22, as said below
Outputs:
- orthonormal: float32 [131072, 128], P(('wide', 'narrow'))
Inputs may be any that keep to these rules, and one draw needn't show every extreme that they name: Slots 0 to counts[w, n] - 1 of device (w, n) hold its tiles, the others are unused; some device has all 22 slots live.
All inputs are finite; a program needn't handle non-finite values.
Results may differ from a plain program's by a relative error of at most 0.0036.
Values may be sent and summed in bfloat16 or wider, within the bound.
No kernel may reach another device: no remote copies, remote signals or barrier semaphores. Data moves between devices by JAX's collectives and lax.ppermute only.
A program may use at most 64 MiB of HBM per device.

v0:
```python
import jax
import jax.numpy as jnp
from jax import lax
from jax.sharding import PartitionSpec as P


def apply_operator(values_bf, tile_local, row_local, col_local, live_count):
    tile_size = tile_local.shape[1]
    width = values_bf.shape[1]
    rows_dev = values_bf.shape[0]
    slab_count = lax.axis_size("narrow") * rows_dev // tile_size
    slot_count = tile_local.shape[0]
    gathered = lax.all_gather(values_bf, "wide", axis=0, tiled=True)
    blocks = gathered.reshape(-1, tile_size, width)
    picked = jnp.take(blocks, col_local, axis=0)
    products = jnp.einsum("sij,sjk->sik", tile_local, picked, preferred_element_type=jnp.float32)
    slot_ids = jnp.arange(slot_count, dtype=jnp.int32)
    slab_ids = jnp.arange(slab_count, dtype=jnp.int32)
    onehot = ((row_local[None, :] == slab_ids[:, None]) & (slot_ids[None, :] < live_count)).astype(
        jnp.float32
    )
    partial_value = jnp.einsum("rs,sik->rik", onehot, products, precision=lax.Precision.HIGHEST)
    partial_value = partial_value.reshape(slab_count * tile_size, width)
    slab_total = lax.psum(partial_value, "narrow")
    return lax.dynamic_slice_in_dim(slab_total, lax.axis_index("narrow") * rows_dev, rows_dev, 0)


def local(embedding, tile_blocks, tile_row, tile_col, counts):
    tile_local = tile_blocks[0, 0]
    row_local = tile_row[0, 0]
    col_local = tile_col[0, 0]
    live_count = counts[0, 0]
    emb_bf = embedding.astype(jnp.bfloat16)
    first_order = apply_operator(emb_bf, tile_local, row_local, col_local, live_count)
    first_bf = first_order.astype(jnp.bfloat16)
    second = (
        2.0 * apply_operator(first_bf, tile_local, row_local, col_local, live_count) - embedding
    )
    spectral = 1.2661 * embedding - 1.1303 * first_order + 0.2715 * second
    gram_part = lax.dot_general(
        spectral, spectral, (((0,), (0,)), ((), ())), precision=lax.Precision.HIGHEST
    )
    gram_matrix = lax.psum(gram_part, ("wide", "narrow"))
    lower_factor = jnp.linalg.cholesky(gram_matrix)
    solved = jax.scipy.linalg.solve_triangular(lower_factor, spectral.T, lower=True)
    node_total = embedding.shape[0] * lax.axis_size("wide") * lax.axis_size("narrow")
    return solved.T * jnp.sqrt(jnp.float32(node_total))


def solution(mesh):
    placed = (
        P(("wide", "narrow"), None),
        P("wide", "narrow", None, None, None),
        P("wide", "narrow", None),
        P("wide", "narrow", None),
        P("wide", "narrow"),
    )
    return jax.shard_map(
        local, mesh=mesh, in_specs=placed, out_specs=P(("wide", "narrow"), None), check_vma=False
    )
```

profile of v0, /device:TPU:1, one launch (start us, length us, event | category | flops | bytes accessed | tf_op | source)
XLA Modules:
  0.0 617.0 jit_solution(5770539556316250015)
XLA Ops:
  6.5 0.0 all-gather.3.cloned.1.call-start
  6.5 1.6 convert_element_type.8
  8.2 0.0 all-gather.3.cloned.1.call-update
  8.2 0.0 all-reduce.4.cloned.1.call-start
  8.9 0.7 compare_select_fusion
  9.6 0.7 compare_and_fusion
  10.2 87.1 %all-gather.3.cloned.1.call-done = bf16[32768,128]{1,0:T(8,128)(2,1)} async-done(((bf16[512,128]{1,0:T(8,128)(2,1)}), bf16[32768,128]{1,0:T(8,128)(2,1)}) %all-gather.3.cloned.1.call-update) | async-done | bytes 8388624 | tf_op jit(solution)/shard_map/all_gather | solution.py:13
  97.3 4.5 gather_fusion
  101.8 11.3 %fusion.2 = f32[22,128,512]{2,1,0:T(8,128)} fusion(bf16[1,1,22,512,512]{4,3,2,1,0:T(8,128)(2,1)} %param.8, bf16[22,512,128]{2,1,0:T(8,128)(2,1)S(1)} %gather_fusion, pred[22]{0:T(512)(128)(4,1)S(1)} %compare_and_fusion), kind=kOutput, calls=%fused_computation.4 | convolution fusion | flops 1477836800 | bytes 20185110 | tf_op jit(solution)/shard_map/sij,sjk->sik/dot_general | solution.py:16
  113.1 0.0 copy-start.1
  113.1 6.5 %copy.12 = f32[22,128,512]{1,0,2:T(8,128)} copy(f32[22,128,512]{2,1,0:T(8,128)} %fusion.2) | data formatting | bytes 11534336 | tf_op jit(solution)/shard_map/sij,sjk->sik/dot_general | solution.py:16
  119.6 0.0 copy-done.1
  119.6 5.0 fusion.6
  124.6 1.0 copy.8
  125.6 0.0 all-reduce.4.cloned.1.call-update
  125.6 0.0 all-gather.5.cloned.1.call-start
  125.7 45.8 %all-reduce.4.cloned.1.call-done = f32[2048,128]{1,0:T(8,128)} async-done(((f32[2048,128]{1,0:T(8,128)}), f32[2048,128]{1,0:T(8,128)}) %all-reduce.4.cloned.1.call-update) | async-done | bytes 1048592 | tf_op jit(solution)/shard_map/psum | solution.py:24
  171.5 1.6 dynamic-slice_convert_fusion
  173.2 0.0 all-gather.5.cloned.1.call-update
  173.2 0.2 all-reduce.6.cloned.1.call-start
  173.4 87.1 %all-gather.5.cloned.1.call-done = bf16[32768,128]{1,0:T(8,128)(2,1)} async-done(((bf16[512,128]{1,0:T(8,128)(2,1)}), bf16[32768,128]{1,0:T(8,128)(2,1)}) %all-gather.5.cloned.1.call-update) | async-done | bytes 8388624 | tf_op jit(solution)/shard_map/all_gather | solution.py:13
  260.5 4.5 gather_fusion.1
  265.0 11.3 %fusion = f32[22,128,512]{2,1,0:T(8,128)} fusion(bf16[1,1,22,512,512]{4,3,2,1,0:T(8,128)(2,1)} %param.8, bf16[22,512,128]{2,1,0:T(8,128)(2,1)S(1)} %gather_fusion.1, pred[22]{0:T(512)(128)(4,1)S(1)} %compare_and_fusion), kind=kOutput, calls=%fused_computation.2 | convolution fusion | flops 1477836800 | bytes 20185110 | tf_op jit(solution)/shard_map/sij,sjk->sik/dot_general | solution.py:16
  276.3 6.4 %copy.13 = f32[22,128,512]{1,0,2:T(8,128)} copy(f32[22,128,512]{2,1,0:T(8,128)} %fusion) | data formatting | bytes 11534336 | tf_op jit(solution)/shard_map/sij,sjk->sik/dot_general | solution.py:16
  282.7 0.0 copy-start
  282.7 5.1 fusion.4
  287.8 1.1 copy.9
  288.9 0.0 all-reduce.6.cloned.1.call-update
  288.9 0.3 all-reduce.8.cloned.1.call-start
  289.2 45.6 %all-reduce.6.cloned.1.call-done = f32[2048,128]{1,0:T(8,128)} async-done(((f32[2048,128]{1,0:T(8,128)}), f32[2048,128]{1,0:T(8,128)}) %all-reduce.6.cloned.1.call-update) | async-done | bytes 1048592 | tf_op jit(solution)/shard_map/psum | solution.py:24
  334.8 0.0 copy-done
  334.8 1.1 multiply_add_fusion
  335.9 1.2 fusion.23
  337.1 0.0 all-reduce.8.cloned.1.call-update
  337.1 247.6 %all-reduce.8.cloned.1.call-done = f32[128,128]{0,1:T(8,128)} async-done(((f32[128,128]{0,1:T(8,128)}), f32[128,128]{0,1:T(8,128)}) %all-reduce.8.cloned.1.call-update) | async-done | bytes 65552 | tf_op jit(solution)/shard_map/psum | solution.py:43
  584.7 0.9 copy.11
  585.6 0.9 fusion.16
  586.5 11.7 %cholesky.16 = f32[128,128]{1,0:T(8,128)S(1)} custom-call(f32[128,128]{1,0:T(8,128)S(1)} %fusion.16), custom_call_target="Cholesky" | custom-call | tf_op jit(solution)/shard_map/jit(cholesky)/cholesky | solution.py:44
  598.2 0.6 compare_reduce_fusion
  598.9 0.7 fusion.14
  599.5 9.8 %custom-call.7 = f32[1,128,128]{1,2,0:T(8,128)S(1)} custom-call(f32[1,128,128]{2,1,0:T(8,128)S(1)} %fusion.14), custom_call_target="InvertDiagBlocksLowerTriangular" | custom-call | tf_op jit(solution)/shard_map/jit(_solve_triangular)/triangular_solve | solution.py:45
  609.4 1.1 convolution_multiply_fusion
  (3 shorter events, 0.1 us)
Async XLA Ops:
  6.5 90.8 %all-gather.3.cloned.1.call-start = ((), (), s32[]{:S(2)}) async-start(), calls=%async_computation | async-start | bytes 8519680 | tf_op jit(solution)/shard_map/all_gather | solution.py:13
  8.2 163.4 %all-reduce.4.cloned.1.call-start = ((), (), s32[]{:S(2)}) async-start(), calls=%async_computation.1 | async-start | bytes 2097152 | tf_op jit(solution)/shard_map/psum | solution.py:24
  113.1 6.5 %copy-start.1 = (s32[1,1,22]{2,1,0:T(1,128)S(1)}, s32[1,1,22]{2,1,0:T(1,128)}, u32[]{:S(2)}) copy-start(s32[1,1,22]{2,1,0:T(1,128)} %param.9) | copy-start | bytes 268
  125.6 134.9 %all-gather.5.cloned.1.call-start = ((), (), s32[]{:S(2)}) async-start(), calls=%async_computation.2 | async-start | bytes 8519680 | tf_op jit(solution)/shard_map/all_gather | solution.py:13
  173.2 161.6 %all-reduce.6.cloned.1.call-start = ((), (), s32[]{:S(2)}) async-start(), calls=%async_computation.3 | async-start | bytes 2097152 | tf_op jit(solution)/shard_map/psum | solution.py:24
  282.7 52.1 %copy-start = (f32[512,128]{1,0:T(8,128)S(1)}, f32[512,128]{1,0:T(8,128)}, u32[]{:S(2)}) copy-start(f32[512,128]{1,0:T(8,128)} %param.7) | copy-start | bytes 786436
  288.9 295.8 %all-reduce.8.cloned.1.call-start = ((), (), s32[]{:S(2)}) async-start(), calls=%async_computation.4 | async-start | bytes 131072 | tf_op jit(solution)/shard_map/psum | solution.py:43
Sparse Core Ops, SparseCore 0:
  10.1 87.1 all-gather.2
  125.8 45.7 all-reduce.3
  174.3 86.1 all-gather.4
  289.0 45.7 all-reduce.5
  340.1 244.5 all-reduce.7
where the time goes:
time: 618 us; the launch traced here: 617 us
  waiting for transfers between devices  513 us (83%)
  matrix products  34.9 us (6%)
  other arithmetic  27.8 us (4%)
  local copies, waits for them, and re-layouts  26.5 us (4%)
  between operations  13.9 us (2%)
    psum x1, waiting for transfers between devices, local(): gram_matrix = lax.psum(gram_part, ('wide', 'narrow'))  248 us
    all_gather x2, waiting for transfers between devices, apply_operator(): gathered = lax.all_gather(values_bf, 'wide', axis=0, tiled=True)  174 us
    psum x2, waiting for transfers between devices, apply_operator(): slab_total = lax.psum(partial_value, 'narrow')  91.4 us
    dot_general x2, matrix products, apply_operator(): jnp.einsum('sij,sjk->sik', tile_local, picked, preferred_element_type=jnp...  22.5 us
    dot_general x2, local copies, waits for them, and re-layouts, apply_operator(): jnp.einsum('sij,sjk->sik', tile_local, picked, preferred_element_type=jnp...  12.9 us
    another operation x3, other arithmetic, local(): lower_factor = jnp.linalg.cholesky(gram_matrix)  12.4 us
  transfers between devices with their start and end apart: 5, of which 5 were waited for; matrix products, arithmetic and copies ran while one was open for 0% of the time, Pallas kernels for 0%

commit v1 on v0

--- a/solution.py
+++ b/solution.py
@@ -40,7 +40,7 @@
     gram_part = lax.dot_general(
         spectral, spectral, (((0,), (0,)), ((), ())), precision=lax.Precision.HIGHEST
     )
-    gram_matrix = lax.psum(gram_part, ("wide", "narrow"))
+    gram_matrix = lax.psum(lax.psum(gram_part, "wide"), "narrow")
     lower_factor = jnp.linalg.cholesky(gram_matrix)
     solved = jax.scipy.linalg.solve_triangular(lower_factor, spectral.T, lower=True)
     node_total = embedding.shape[0] * lax.axis_size("wide") * lax.axis_size("narrow")

time: 618 us -> 589 us (0.953)
  waiting for transfers between devices: 513 us -> 483 us
    psum x1 -> x2, waiting for transfers between devices: 248 us -> 217 us  [local(): gram_matrix = lax.psum(lax.psum(gram_part, 'wide'), 'narrow')]
  transfers between devices with their start and end apart: 5 -> 6, of which waited for: 5 -> 6; matrix products, arithmetic and copies ran while one was open for 0% -> 0% of each run, Pallas kernels for 0% -> 0%
where the time goes in v1:
time: 589 us; the launch traced here: 587 us
  waiting for transfers between devices  483 us (82%)
  matrix products  34.9 us (6%)
  other arithmetic  27.8 us (5%)
  local copies, waits for them, and re-layouts  26.5 us (4%)
  between operations  14.2 us (2%)
    psum x2, waiting for transfers between devices, local(): gram_matrix = lax.psum(lax.psum(gram_part, 'wide'), 'narrow')  217 us
    all_gather x2, waiting for transfers between devices, apply_operator(): gathered = lax.all_gather(values_bf, 'wide', axis=0, tiled=True)  174 us
    psum x2, waiting for transfers between devices, apply_operator(): slab_total = lax.psum(partial_value, 'narrow')  91.7 us
    dot_general x2, matrix products, apply_operator(): jnp.einsum('sij,sjk->sik', tile_local, picked, preferred_element_type=jnp...  22.5 us
    dot_general x2, local copies, waits for them, and re-layouts, apply_operator(): jnp.einsum('sij,sjk->sik', tile_local, picked, preferred_element_type=jnp...  12.9 us
    another operation x3, other arithmetic, local(): lower_factor = jnp.linalg.cholesky(gram_matrix)  12.4 us
  transfers between devices with their start and end apart: 6, of which 6 were waited for; matrix products, arithmetic and copies ran while one was open for 0% of the time, Pallas kernels for 0%

profile of v1, /device:TPU:1, one launch (start us, length us, event | category | flops | bytes accessed | tf_op | source)
XLA Modules:
  0.0 587.5 jit_solution(11351835693604825393)
XLA Ops:
  6.5 0.0 all-gather.3.cloned.1.call-start
  6.5 1.6 convert_element_type.8
  8.2 0.0 all-gather.3.cloned.1.call-update
  8.2 0.0 all-reduce.5.cloned.1.call-start
  8.9 0.7 compare_select_fusion
  9.6 0.7 compare_and_fusion
  10.2 87.1 %all-gather.3.cloned.1.call-done = bf16[32768,128]{1,0:T(8,128)(2,1)} async-done(((bf16[512,128]{1,0:T(8,128)(2,1)}), bf16[32768,128]{1,0:T(8,128)(2,1)}) %all-gather.3.cloned.1.call-update) | async-done | bytes 8388624 | tf_op jit(solution)/shard_map/all_gather | solution.py:13
  97.3 4.5 gather_fusion
  101.8 11.3 %fusion.2 = f32[22,128,512]{2,1,0:T(8,128)} fusion(bf16[1,1,22,512,512]{4,3,2,1,0:T(8,128)(2,1)} %param.8, bf16[22,512,128]{2,1,0:T(8,128)(2,1)S(1)} %gather_fusion, pred[22]{0:T(512)(128)(4,1)S(1)} %compare_and_fusion), kind=kOutput, calls=%fused_computation.4 | convolution fusion | flops 1477836800 | bytes 20185110 | tf_op jit(solution)/shard_map/sij,sjk->sik/dot_general | solution.py:16
  113.1 0.0 copy-start.1
  113.1 6.5 %copy.12 = f32[22,128,512]{1,0,2:T(8,128)} copy(f32[22,128,512]{2,1,0:T(8,128)} %fusion.2) | data formatting | bytes 11534336 | tf_op jit(solution)/shard_map/sij,sjk->sik/dot_general | solution.py:16
  119.6 0.0 copy-done.1
  119.6 5.0 fusion.6
  124.6 1.0 copy.8
  125.6 0.0 all-reduce.5.cloned.1.call-update
  125.6 0.0 all-gather.5.cloned.1.call-start
  125.7 45.8 %all-reduce.5.cloned.1.call-done = f32[2048,128]{1,0:T(8,128)} async-done(((f32[2048,128]{1,0:T(8,128)}), f32[2048,128]{1,0:T(8,128)}) %all-reduce.5.cloned.1.call-update) | async-done | bytes 1048592 | tf_op jit(solution)/shard_map/psum | solution.py:24
  171.5 1.6 dynamic-slice_convert_fusion
  173.2 0.0 all-gather.5.cloned.1.call-update
  173.2 0.2 all-reduce.7.cloned.1.call-start
  173.4 87.1 %all-gather.5.cloned.1.call-done = bf16[32768,128]{1,0:T(8,128)(2,1)} async-done(((bf16[512,128]{1,0:T(8,128)(2,1)}), bf16[32768,128]{1,0:T(8,128)(2,1)}) %all-gather.5.cloned.1.call-update) | async-done | bytes 8388624 | tf_op jit(solution)/shard_map/all_gather | solution.py:13
  260.5 4.5 gather_fusion.1
  265.0 11.3 %fusion = f32[22,128,512]{2,1,0:T(8,128)} fusion(bf16[1,1,22,512,512]{4,3,2,1,0:T(8,128)(2,1)} %param.8, bf16[22,512,128]{2,1,0:T(8,128)(2,1)S(1)} %gather_fusion.1, pred[22]{0:T(512)(128)(4,1)S(1)} %compare_and_fusion), kind=kOutput, calls=%fused_computation.2 | convolution fusion | flops 1477836800 | bytes 20185110 | tf_op jit(solution)/shard_map/sij,sjk->sik/dot_general | solution.py:16
  276.3 6.4 %copy.13 = f32[22,128,512]{1,0,2:T(8,128)} copy(f32[22,128,512]{2,1,0:T(8,128)} %fusion) | data formatting | bytes 11534336 | tf_op jit(solution)/shard_map/sij,sjk->sik/dot_general | solution.py:16
  282.7 0.0 copy-start
  282.7 5.1 fusion.4
  287.8 1.1 copy.9
  288.9 0.0 all-reduce.7.cloned.1.call-update
  288.9 0.0 all-reduce.9.cloned.1.call-start
  289.0 45.8 %all-reduce.7.cloned.1.call-done = f32[2048,128]{1,0:T(8,128)} async-done(((f32[2048,128]{1,0:T(8,128)}), f32[2048,128]{1,0:T(8,128)}) %all-reduce.7.cloned.1.call-update) | async-done | bytes 1048592 | tf_op jit(solution)/shard_map/psum | solution.py:24
  334.8 0.0 copy-done
  334.8 1.1 multiply_add_fusion
  335.9 1.2 fusion.23
  337.1 0.0 all-reduce.9.cloned.1.call-update
  337.1 0.3 all-reduce.11.cloned.1.call-start
  337.4 174.4 %all-reduce.9.cloned.1.call-done = f32[128,128]{0,1:T(8,128)} async-done(((f32[128,128]{0,1:T(8,128)}), f32[128,128]{0,1:T(8,128)}) %all-reduce.9.cloned.1.call-update) | async-done | bytes 65552 | tf_op jit(solution)/shard_map/psum | solution.py:43
  511.8 0.0 all-reduce.11.cloned.1.call-update
  511.8 43.1 %all-reduce.11.cloned.1.call-done = f32[128,128]{0,1:T(8,128)} async-done(((f32[128,128]{0,1:T(8,128)}), f32[128,128]{0,1:T(8,128)}) %all-reduce.11.cloned.1.call-update) | async-done | bytes 65552 | tf_op jit(solution)/shard_map/psum | solution.py:43
  554.9 0.9 copy.11
  555.8 0.9 fusion.16
  556.7 11.7 %cholesky.16 = f32[128,128]{1,0:T(8,128)S(1)} custom-call(f32[128,128]{1,0:T(8,128)S(1)} %fusion.16), custom_call_target="Cholesky" | custom-call | tf_op jit(solution)/shard_map/jit(cholesky)/cholesky | solution.py:44
  568.5 0.6 compare_reduce_fusion
  569.1 0.7 fusion.14
  569.8 9.8 %custom-call.7 = f32[1,128,128]{1,2,0:T(8,128)S(1)} custom-call(f32[1,128,128]{2,1,0:T(8,128)S(1)} %fusion.14), custom_call_target="InvertDiagBlocksLowerTriangular" | custom-call | tf_op jit(solution)/shard_map/jit(_solve_triangular)/triangular_solve | solution.py:45
  579.6 1.1 convolution_multiply_fusion
  (3 shorter events, 0.1 us)
Async XLA Ops:
  6.5 90.8 %all-gather.3.cloned.1.call-start = ((), (), s32[]{:S(2)}) async-start(), calls=%async_computation | async-start | bytes 8519680 | tf_op jit(solution)/shard_map/all_gather | solution.py:13
  8.2 163.4 %all-reduce.5.cloned.1.call-start = ((), (), s32[]{:S(2)}) async-start(), calls=%async_computation.1 | async-start | bytes 2097152 | tf_op jit(solution)/shard_map/psum | solution.py:24
  113.1 6.5 %copy-start.1 = (s32[1,1,22]{2,1,0:T(1,128)S(1)}, s32[1,1,22]{2,1,0:T(1,128)}, u32[]{:S(2)}) copy-start(s32[1,1,22]{2,1,0:T(1,128)} %param.9) | copy-start | bytes 268
  125.6 134.9 %all-gather.5.cloned.1.call-start = ((), (), s32[]{:S(2)}) async-start(), calls=%async_computation.2 | async-start | bytes 8519680 | tf_op jit(solution)/shard_map/all_gather | solution.py:13
  173.2 161.6 %all-reduce.7.cloned.1.call-start = ((), (), s32[]{:S(2)}) async-start(), calls=%async_computation.3 | async-start | bytes 2097152 | tf_op jit(solution)/shard_map/psum | solution.py:24
  282.7 52.1 %copy-start = (f32[512,128]{1,0:T(8,128)S(1)}, f32[512,128]{1,0:T(8,128)}, u32[]{:S(2)}) copy-start(f32[512,128]{1,0:T(8,128)} %param.7) | copy-start | bytes 786436
  288.9 222.9 %all-reduce.9.cloned.1.call-start = ((), (), s32[]{:S(2)}) async-start(), calls=%async_computation.4 | async-start | bytes 131072 | tf_op jit(solution)/shard_map/psum | solution.py:43
  337.1 217.8 %all-reduce.11.cloned.1.call-start = ((), (), s32[]{:S(2)}) async-start(), calls=%async_computation.5 | async-start | bytes 131072 | tf_op jit(solution)/shard_map/psum | solution.py:43
Sparse Core Ops, SparseCore 0:
  10.1 87.1 all-gather.2
  125.8 45.7 all-reduce.4
  174.3 86.1 all-gather.4
  289.0 45.7 all-reduce.6
  338.1 173.6 all-reduce.8
  514.0 40.8 all-reduce.10

commit v2 on v0

--- a/solution.py
+++ b/solution.py
@@ -10,7 +10,9 @@
     rows_dev = values_bf.shape[0]
     slab_count = lax.axis_size("narrow") * rows_dev // tile_size
     slot_count = tile_local.shape[0]
-    gathered = lax.all_gather(values_bf, "wide", axis=0, tiled=True)
+    gathered = jnp.concatenate(
+        lax.all_to_all(jnp.stack([values_bf] * lax.axis_size("wide")), "wide", 0, 0), axis=0
+    )
     blocks = gathered.reshape(-1, tile_size, width)
     picked = jnp.take(blocks, col_local, axis=0)
     products = jnp.einsum("sij,sjk->sik", tile_local, picked, preferred_element_type=jnp.float32)

time: 618 us -> 845 us (1.37)
  blocking collectives: 0 us -> 198 us
  starting transfers between devices: 0.57 us -> 13.8 us
  waiting for transfers between devices: 513 us -> 524 us
    all_to_all x0 -> x1, blocking collectives: none -> 198 us  [apply_operator(): lax.all_to_all(jnp.stack([values_bf] * lax.axis_size('wide')), 'wide', 0, 0)]
    all_to_all x0 -> x1, waiting for transfers between devices: none -> 185 us  [apply_operator(): lax.all_to_all(jnp.stack([values_bf] * lax.axis_size('wide')), 'wide', 0, 0)]
    all_gather x2 -> x0, waiting for transfers between devices: 174 us -> none  [apply_operator(): gathered = lax.all_gather(values_bf, 'wide', axis=0, tiled=True)]
    all_to_all x0 -> x1, starting transfers between devices: none -> 13.5 us  [apply_operator(): lax.all_to_all(jnp.stack([values_bf] * lax.axis_size('wide')), 'wide', 0, 0)]
  transfers between devices with their start and end apart: 5 -> 4, of which waited for: 5 -> 4; matrix products, arithmetic and copies ran while one was open for 0% -> 0% of each run, Pallas kernels for 0% -> 0%
where the time goes in v2:
time: 845 us; the launch traced here: 844 us
  waiting for transfers between devices  524 us (62%)
  blocking collectives  198 us (23%)
  matrix products  34.9 us (4%)
  local copies, waits for them, and re-layouts  33.2 us (4%)
  other arithmetic  25.8 us (3%)
  between operations  13.9 us (2%)
  starting transfers between devices  13.8 us (2%)
    psum x1, waiting for transfers between devices, local(): gram_matrix = lax.psum(gram_part, ('wide', 'narrow'))  248 us
    all_to_all x1, blocking collectives, apply_operator(): lax.all_to_all(jnp.stack([values_bf] * lax.axis_size('wide')), 'wide', 0, 0)  198 us
    all_to_all x1, waiting for transfers between devices, apply_operator(): lax.all_to_all(jnp.stack([values_bf] * lax.axis_size('wide')), 'wide', 0, 0)  185 us
    psum x2, waiting for transfers between devices, apply_operator(): slab_total = lax.psum(partial_value, 'narrow')  91.4 us
    dot_general x2, matrix products, apply_operator(): jnp.einsum('sij,sjk->sik', tile_local, picked, preferred_element_type=jnp...  22.6 us
  transfers between devices with their start and end apart: 4, of which 4 were waited for; matrix products, arithmetic and copies ran while one was open for 0% of the time, Pallas kernels for 0%

profile of v2, /device:TPU:1, one launch (start us, length us, event | category | flops | bytes accessed | tf_op | source)
XLA Modules:
  0.0 844.1 jit_solution(16549925327088196718)
XLA Ops:
  6.5 1.0 convert_element_type.8
  7.5 5.2 stack.4
  12.7 0.0 copy-start.2
  12.7 13.5 %all-to-all-start = ((bf16[64,512,128]{2,1,0:T(8,128)(2,1)}), bf16[64,512,128]{2,1,0:T(8,128)(2,1)}, u32[]{:S(2)}, u32[]{:S(2)}) async-start(bf16[64,512,128]{2,1,0:T(8,128)(2,1)} %stack.4), calls=%async_computation | async-start | bytes 16777216 | tf_op jit(solution)/shard_map/all_to_all | solution.py:14
  26.2 0.0 all-reduce.4.cloned.1.call-start
  26.9 0.0 copy-done.2
  27.0 185.0 %all-to-all-done = bf16[64,512,128]{2,1,0:T(8,128)(2,1)} async-done(((bf16[64,512,128]{2,1,0:T(8,128)(2,1)}), bf16[64,512,128]{2,1,0:T(8,128)(2,1)}, u32[]{:S(2)}, u32[]{:S(2)}) %all-to-all-start) | async-done | bytes 8388640 | tf_op jit(solution)/shard_map/all_to_all | solution.py:14
  211.9 4.5 gather_fusion
  216.4 11.3 %fusion.2 = f32[22,128,512]{2,1,0:T(8,128)} fusion(bf16[1,1,22,512,512]{4,3,2,1,0:T(8,128)(2,1)} %param.8, bf16[22,512,128]{2,1,0:T(8,128)(2,1)S(1)} %gather_fusion, pred[22]{0:T(512)(128)(4,1)S(1)} %compare_and_fusion), kind=kOutput, calls=%fused_computation.4 | convolution fusion | flops 1477836800 | bytes 20185110 | tf_op jit(solution)/shard_map/sij,sjk->sik/dot_general | solution.py:18
  227.7 0.0 copy-start.1
  227.7 6.5 copy.12
  234.2 0.0 copy-done.1
  234.2 5.0 fusion.6
  239.2 1.1 copy.8
  240.3 0.0 all-reduce.4.cloned.1.call-update
  240.3 0.0 all-reduce.6.cloned.1.call-start
  240.4 46.0 %all-reduce.4.cloned.1.call-done = f32[2048,128]{1,0:T(8,128)} async-done(((f32[2048,128]{1,0:T(8,128)}), f32[2048,128]{1,0:T(8,128)}) %all-reduce.4.cloned.1.call-update) | async-done | bytes 1048592 | tf_op jit(solution)/shard_map/psum | solution.py:26
  286.3 1.0 dynamic-slice_convert_fusion
  287.3 2.0 stack.5
  289.3 198.4 %all_to_all.10 = bf16[64,512,128]{2,1,0:T(8,128)(2,1)} all-to-all(bf16[64,512,128]{2,1,0:T(8,128)(2,1)S(1)} %stack.5), channel_id=1, replica_groups=mesh['wide'=64,'narrow'=4] {'wide'}, dimensions={0} | all-to-all | bytes 16777216 | tf_op jit(solution)/shard_map/all_to_all | solution.py:14
  487.7 4.5 gather_fusion.1
  492.2 11.3 %fusion = f32[22,128,512]{2,1,0:T(8,128)} fusion(bf16[1,1,22,512,512]{4,3,2,1,0:T(8,128)(2,1)} %param.8, bf16[22,512,128]{2,1,0:T(8,128)(2,1)S(1)} %gather_fusion.1, pred[22]{0:T(512)(128)(4,1)S(1)} %compare_and_fusion), kind=kOutput, calls=%fused_computation.2 | convolution fusion | flops 1477836800 | bytes 20185110 | tf_op jit(solution)/shard_map/sij,sjk->sik/dot_general | solution.py:18
  503.5 6.5 copy.13
  510.0 0.0 copy-start
  510.0 5.1 fusion.4
  515.0 1.1 copy.9
  516.1 0.0 all-reduce.6.cloned.1.call-update
  516.2 0.3 all-reduce.8.cloned.1.call-start
  516.4 45.4 %all-reduce.6.cloned.1.call-done = f32[2048,128]{1,0:T(8,128)} async-done(((f32[2048,128]{1,0:T(8,128)}), f32[2048,128]{1,0:T(8,128)}) %all-reduce.6.cloned.1.call-update) | async-done | bytes 1048592 | tf_op jit(solution)/shard_map/psum | solution.py:26
  561.8 0.0 copy-done
  561.8 1.1 multiply_add_fusion
  562.9 1.2 fusion.23
  564.1 0.0 all-reduce.8.cloned.1.call-update
  564.2 247.7 %all-reduce.8.cloned.1.call-done = f32[128,128]{0,1:T(8,128)} async-done(((f32[128,128]{0,1:T(8,128)}), f32[128,128]{0,1:T(8,128)}) %all-reduce.8.cloned.1.call-update) | async-done | bytes 65552 | tf_op jit(solution)/shard_map/psum | solution.py:45
  811.8 0.9 copy.11
  812.8 0.9 fusion.16
  813.6 11.7 %cholesky.16 = f32[128,128]{1,0:T(8,128)S(1)} custom-call(f32[128,128]{1,0:T(8,128)S(1)} %fusion.16), custom_call_target="Cholesky" | custom-call | tf_op jit(solution)/shard_map/jit(cholesky)/cholesky | solution.py:46
  825.4 0.6 compare_reduce_fusion
  826.0 0.7 fusion.14
  826.7 9.8 %custom-call.7 = f32[1,128,128]{1,2,0:T(8,128)S(1)} custom-call(f32[1,128,128]{2,1,0:T(8,128)S(1)} %fusion.14), custom_call_target="InvertDiagBlocksLowerTriangular" | custom-call | tf_op jit(solution)/shard_map/jit(_solve_triangular)/triangular_solve | solution.py:47
  836.5 1.1 convolution_multiply_fusion
  (5 shorter events, 0.1 us)
Async XLA Ops:
  12.7 14.2 %copy-start.2 = (s32[1,1,22]{2,1,0:T(1,128)S(1)}, s32[1,1,22]{2,1,0:T(1,128)}, u32[]{:S(2)}) copy-start(s32[1,1,22]{2,1,0:T(1,128)} %param.10) | copy-start | bytes 268
  12.7 199.2 %all-to-all-start = ((bf16[64,512,128]{2,1,0:T(8,128)(2,1)}), bf16[64,512,128]{2,1,0:T(8,128)(2,1)}, u32[]{:S(2)}, u32[]{:S(2)}) async-start(bf16[64,512,128]{2,1,0:T(8,128)(2,1)} %stack.4), calls=%async_computation | async-start | bytes 16777216 | tf_op jit(solution)/shard_map/all_to_all | solution.py:14
  26.2 260.1 %all-reduce.4.cloned.1.call-start = ((), (), s32[]{:S(2)}) async-start(), calls=%async_computation.2 | async-start | bytes 2097152 | tf_op jit(solution)/shard_map/psum | solution.py:26
  227.7 6.5 copy-start.1
  240.3 321.5 %all-reduce.6.cloned.1.call-start = ((), (), s32[]{:S(2)}) async-start(), calls=%async_computation.3 | async-start | bytes 2097152 | tf_op jit(solution)/shard_map/psum | solution.py:26
  510.0 51.8 %copy-start = (f32[512,128]{1,0:T(8,128)S(1)}, f32[512,128]{1,0:T(8,128)}, u32[]{:S(2)}) copy-start(f32[512,128]{1,0:T(8,128)} %param.7) | copy-start | bytes 786436
  516.2 295.7 %all-reduce.8.cloned.1.call-start = ((), (), s32[]{:S(2)}) async-start(), calls=%async_computation.4 | async-start | bytes 131072 | tf_op jit(solution)/shard_map/psum | solution.py:45
Sparse Core Ops, SparseCore 0:
  240.4 45.8 all-reduce.3
  516.3 45.4 all-reduce.5
  567.3 244.4 all-reduce.7
